TPU v7x, 256 devices: a whole 4x4x8 slice. The times are simulated.
256 devices in a mesh: ab: 64 (over z, y, core), cd: 4 (over x).
Axes of the slice: x: 4, y: 4, z: 8, core: 2. Of those that a mesh axis runs over, the one named last changes fastest.
Arguments:
- t2_amps: float32 [1024, 8192], P('ab', 'cd'), may hold values from -6 to 6
- v_slab: float32 [65536, 8192], P('ab', 'cd'), may hold values from -0.1875 to 0.1875
- ij_irrep: int32 [1024], P('ab'), may hold values from 0 to 7, as said below
- ab_irrep: int32 [65536], P('ab'), may hold values from 0 to 7, as said below
- cd_irrep: int32 [8192], P('cd'), may hold values from 0 to 7, as said below
Outputs:
- ladder: float32 [1024, 65536], P(('ab', 'cd'))
Inputs may be any that keep to these rules, and one draw needn't show every extreme that they name: `ij_irrep`: irrep labels of D2h in any order and any counts; a pair couples only to pairs of the same label. All occupied pairs of one device may carry one label. `ab_irrep`: irrep labels of D2h in any order and any counts; all pairs of one device may carry one label. `cd_irrep`: irrep labels of D2h in any order and any counts; all pairs of one device may carry one label.
All inputs are finite; a program needn't handle non-finite values.
Results may differ from a plain program's by a relative error of at most 0.0003.
Values sent between devices are 32-bit elements; how exact they have to be, the bound alone decides.
A program may use at most 64 MiB of HBM per device.

v0:
```python
import jax
import jax.numpy as jnp
from jax import lax
from jax.sharding import PartitionSpec as P


def on_device(t2_amps, v_slab, ij_irrep, ab_irrep, cd_irrep):
    t2_sym = t2_amps * (ij_irrep[:, None] == cd_irrep[None, :]).astype(t2_amps.dtype)
    v_sym = v_slab * (ab_irrep[:, None] == cd_irrep[None, :]).astype(v_slab.dtype)
    partial_value = lax.dot_general(
        lax.all_gather(t2_sym, "ab", axis=0, tiled=True),
        v_sym,
        (((1,), (1,)), ((), ())),
        precision=lax.Precision.HIGHEST,
        preferred_element_type=jnp.float32,
    )
    n_rows = lax.axis_size("ab")
    n_cols = lax.axis_size("cd")
    width = partial_value.shape[1]
    per_dev = partial_value.shape[0] // (n_rows * n_cols)
    regrouped = partial_value.reshape(n_rows, n_cols, per_dev, width)
    regrouped = jnp.transpose(regrouped, (1, 0, 2, 3)).reshape(partial_value.shape[0], width)
    summed = lax.psum_scatter(regrouped, "cd", scatter_dimension=0, tiled=True)
    ladder = lax.all_to_all(summed, "ab", split_axis=0, concat_axis=1, tiled=True)
    return ladder


def solution(mesh):
    in_specs = (P("ab", "cd"), P("ab", "cd"), P("ab"), P("ab"), P("cd"))
    out_specs = P(("ab", "cd"), None)
    return jax.shard_map(
        on_device, mesh=mesh, in_specs=in_specs, out_specs=out_specs, check_vma=False
    )
```

profile of v0, /device:TPU:1, one launch (start us, length us, event | category | flops | bytes accessed | tf_op | source)
XLA Modules:
  0.0 240.3 jit_solution(217428079767022441)
XLA Ops:
  6.5 0.0 all-gather.2.cloned.1.call-start
  6.5 1.7 compare_select_fusion
  8.2 0.0 all-gather.2.cloned.1.call-update
  8.2 0.0 reduce-scatter.2.cloned.1.call-start
  8.3 89.1 %all-gather.2.cloned.1.call-done = f32[1024,2048]{1,0:T(8,128)} async-done(((f32[16,2048]{1,0:T(8,128)}), f32[1024,2048]{1,0:T(8,128)}) %all-gather.2.cloned.1.call-update) | async-done | bytes 8388624 | tf_op jit(solution)/shard_map/all_gather | solution.py:11
  97.3 33.1 %fusion = f32[1024,1024]{1,0:T(8,128)} fusion(f32[1024,2048]{1,0:T(8,128)} %all-gather.2.cloned.1.call-done, f32[1024,2048]{1,0:T(8,128)} %param.6, s32[2048]{0:T(1024)} %param.9, s32[1024]{0:T(1024)} %param.8), kind=kOutput, calls=%fused_computation | convolution fusion | flops 25773998080 | bytes 20983808 | tf_op jit(solution)/shard_map/dot_general | solution.py:10
  130.4 5.2 %reshape.12 = f32[64,4,4,1024]{3,2,1,0:T(4,128)} reshape(f32[1024,1024]{1,0:T(8,128)} %fusion) | data formatting | bytes 8388608 | tf_op jit(solution)/shard_map/reshape | solution.py:21
  135.6 5.5 %copy.8 = f32[64,4,4,1024]{3,2,0,1:T(4,128)} copy(f32[64,4,4,1024]{3,2,1,0:T(4,128)} %reshape.12) | data formatting | bytes 8388608 | tf_op jit(solution)/shard_map/reshape | solution.py:21
  141.0 5.3 %reshape.13 = f32[1024,1024]{1,0:T(8,128)} reshape(f32[4,64,4,1024]{3,2,1,0:T(4,128)} %bitcast.7) | data formatting | bytes 8388608 | tf_op jit(solution)/shard_map/reshape | solution.py:22
  146.3 0.0 reduce-scatter.2.cloned.1.call-update
  146.4 45.8 %reduce-scatter.2.cloned.1.call-done = f32[256,1024]{1,0:T(8,128)} async-done(((f32[1024,1024]{1,0:T(8,128)}), f32[256,1024]{1,0:T(8,128)}) %reduce-scatter.2.cloned.1.call-update) | async-done | bytes 1048592 | tf_op jit(solution)/shard_map/reduce_scatter | solution.py:23
  192.2 1.5 all_to_all.14
  193.7 38.7 %all_to_all.19 = f32[64,4,1024]{2,1,0:T(4,128)S(1)} all-to-all(f32[64,4,1024]{2,1,0:T(4,128)S(1)} %all_to_all.14), channel_id=1, replica_groups=mesh['ab'=64,'cd'=4] {'ab'}, dimensions={0} | all-to-all | bytes 2097152 | tf_op jit(solution)/shard_map/all_to_all | solution.py:24
  232.4 1.0 copy.10
Async XLA Ops:
  6.5 90.8 %all-gather.2.cloned.1.call-start = ((), (), s32[]{:S(2)}) async-start(), calls=%async_computation.2 | async-start | bytes 8519680 | tf_op jit(solution)/shard_map/all_gather | solution.py:11
  8.2 184.0 %reduce-scatter.2.cloned.1.call-start = ((), (), s32[]{:S(2)}) async-start(), calls=%async_computation.3 | async-start | bytes 5242880 | tf_op jit(solution)/shard_map/reduce_scatter | solution.py:23
Sparse Core Ops, SparseCore 0:
  10.1 87.1 all-gather.1
  146.5 45.6 reduce-scatter.1
where the time goes:
time: 241 us; the launch traced here: 240 us
  waiting for transfers between devices  135 us (56%)
  blocking collectives  38.7 us (16%)
  matrix products  33.1 us (14%)
  local copies, waits for them, and re-layouts  18.4 us (8%)
  between operations  13.4 us (6%)
    all_gather x1, waiting for transfers between devices, on_device(): lax.all_gather(t2_sym, 'ab', axis=0, tiled=True)  89.1 us
    reduce_scatter x1, waiting for transfers between devices, on_device(): summed = lax.psum_scatter(regrouped, 'cd', scatter_dimension=0, tiled=True)  45.8 us
    all_to_all x1, blocking collectives, on_device(): lax.all_to_all(summed, 'ab', split_axis=0, concat_axis=1, tiled=True)  38.7 us
    dot_general x1, matrix products, on_device(): lax.dot_general(lax.all_gather(t2_sym, 'ab', axis=0, tiled=True), v_sym,...  33.1 us
    reshape x2, local copies, waits for them, and re-layouts, on_device(): regrouped = partial_value.reshape(n_rows, n_cols, per_dev, width)  10.6 us
    reshape x1, local copies, waits for them, and re-layouts, on_device(): jnp.transpose(regrouped, (1, 0, 2, 3))  5.29 us
  transfers between devices with their start and end apart: 2, of which 2 were waited for; matrix products, arithmetic and copies ran while one was open for 0% of the time, Pallas kernels for 0%

commit v1 on v0

--- a/solution.py
+++ b/solution.py
@@ -1,14 +1,30 @@
+import functools
 import jax
 import jax.numpy as jnp
 from jax import lax
 from jax.sharding import PartitionSpec as P
 
 
+def _fix_shards(s0, link_axis, at_axis):
+    return jnp.concatenate(
+        lax.all_to_all(
+            jnp.stack([s0] * lax.psum(1, axis_name=link_axis), axis=0),
+            axis_name=link_axis,
+            split_axis=0,
+            concat_axis=0,
+        ),
+        axis=at_axis,
+    )
+
+
+process_rails = functools.partial(_fix_shards, link_axis="ab", at_axis=0)
+
+
 def on_device(t2_amps, v_slab, ij_irrep, ab_irrep, cd_irrep):
     t2_sym = t2_amps * (ij_irrep[:, None] == cd_irrep[None, :]).astype(t2_amps.dtype)
     v_sym = v_slab * (ab_irrep[:, None] == cd_irrep[None, :]).astype(v_slab.dtype)
     partial_value = lax.dot_general(
-        lax.all_gather(t2_sym, "ab", axis=0, tiled=True),
+        process_rails(t2_sym),
         v_sym,
         (((1,), (1,)), ((), ())),
         precision=lax.Precision.HIGHEST,

time: 241 us -> 359 us (1.49)
  blocking collectives: 38.7 us -> 236 us
  waiting for transfers between devices: 135 us -> 47.1 us
  matrix products: 33.1 us -> 42.7 us
    all_to_all x0 -> x1, blocking collectives: none -> 197 us  [_fix_shards(): lax.all_to_all(jnp.stack([s0] * lax.psum(1, axis_name=link_axis), axis=0)...]
    all_gather x1 -> x0, waiting for transfers between devices: 89.1 us -> none  [on_device(): lax.all_gather(t2_sym, 'ab', axis=0, tiled=True)]
    reshape x2 -> x0, local copies, waits for them, and re-layouts: 10.6 us -> none  [on_device(): regrouped = partial_value.reshape(n_rows, n_cols, per_dev, width)]
    dot_general x1, matrix products: 33.1 us -> 42.7 us  [on_device(): lax.dot_general(process_rails(t2_sym), v_sym, (((1,), (1,)), ((), ())), p...]
    all_to_all x0 -> x1, local copies, waits for them, and re-layouts: none -> 4.86 us  [_fix_shards(): lax.all_to_all(jnp.stack([s0] * lax.psum(1, axis_name=link_axis), axis=0)...]
    transpose x0 -> x1, local copies, waits for them, and re-layouts: none -> 4.67 us  [on_device(): jnp.transpose(regrouped, (1, 0, 2, 3))]
  transfers between devices with their start and end apart: 2 -> 1, of which waited for: 2 -> 1; matrix products, arithmetic and copies ran while one was open for 0% -> 0% of each run, Pallas kernels for 0% -> 0%
where the time goes in v1:
time: 359 us
  blocking collectives  236 us (66%)
  waiting for transfers between devices  47.1 us (13%)
  matrix products  42.7 us (12%)
  local copies, waits for them, and re-layouts  18.3 us (5%)
  between operations  13.4 us (4%)
    all_to_all x1, blocking collectives, _fix_shards(): lax.all_to_all(jnp.stack([s0] * lax.psum(1, axis_name=link_axis), axis=0)...  197 us
    reduce_scatter x1, waiting for transfers between devices, on_device(): summed = lax.psum_scatter(regrouped, 'cd', scatter_dimension=0, tiled=True)  47.1 us
    dot_general x1, matrix products, on_device(): lax.dot_general(process_rails(t2_sym), v_sym, (((1,), (1,)), ((), ())), p...  42.7 us
    all_to_all x1, blocking collectives, on_device(): lax.all_to_all(summed, 'ab', split_axis=0, concat_axis=1, tiled=True)  38.7 us
  transfers between devices with their start and end apart: 1, of which 1 were waited for; matrix products, arithmetic and copies ran while one was open for 0% of the time, Pallas kernels for 0%

profile of v1, /device:TPU:1, one launch (start us, length us, event | category | flops | bytes accessed | tf_op | source)
XLA Modules:
  0.0 358.7 jit_solution(4811865304627761373)
XLA Ops:
  6.5 0.0 reduce-scatter.2.cloned.1.call-start
  6.5 1.0 compare_select_fusion
  7.5 1.0 stack.2
  8.6 197.5 %all_to_all.24 = f32[64,16,2048]{2,1,0:T(8,128)S(1)} all-to-all(f32[64,16,2048]{2,1,0:T(8,128)S(1)} %stack.2), channel_id=1, replica_groups=mesh['ab'=64,'cd'=4] {'ab'}, dimensions={0} | all-to-all | bytes 16777216 | tf_op jit(solution)/shard_map/all_to_all | solution.py:10
  206.1 0.0 copy-start
  206.1 0.0 copy-start.1
  206.1 4.9 %copy.7 = f32[64,16,2048]{2,0,1:T(8,128)S(1)} copy(f32[64,16,2048]{2,1,0:T(8,128)S(1)} %all_to_all.24) | data formatting | bytes 16777216 | tf_op jit(solution)/shard_map/all_to_all | solution.py:10
  210.9 0.0 copy-done
  210.9 0.0 copy-done.1
  210.9 42.7 %fusion.7 = f32[4,64,4,1024]{3,1,2,0:T(8,128)S(1)} fusion(f32[64,4,4,2048]{3,0,2,1:T(8,128)S(1)} %bitcast.14, f32[1024,2048]{1,0:T(8,128)} %param.6, s32[2048]{0:T(1024)S(1)} %copy-done, s32[1024]{0:T(1024)S(1)} %copy-done.1), kind=kOutput, calls=%fused_computation.7 | convolution fusion | flops 25773998080 | bytes 20983808 | tf_op jit(solution)/shard_map/dot_general | solution.py:26
  253.6 4.7 %copy.8 = f32[4,64,4,1024]{3,2,1,0:T(4,128)} copy(f32[4,64,4,1024]{3,1,2,0:T(8,128)S(1)} %fusion.7) | data formatting | bytes 8388608 | tf_op jit(solution)/shard_map/transpose | solution.py:38
  258.3 5.3 %reshape.15 = f32[1024,1024]{1,0:T(8,128)} reshape(f32[4,64,4,1024]{3,2,1,0:T(4,128)} %copy.8) | data formatting | bytes 8388608 | tf_op jit(solution)/shard_map/reshape | solution.py:38
  263.6 0.0 reduce-scatter.2.cloned.1.call-update
  263.6 47.1 %reduce-scatter.2.cloned.1.call-done = f32[256,1024]{1,0:T(8,128)} async-done(((f32[1024,1024]{1,0:T(8,128)}), f32[256,1024]{1,0:T(8,128)}) %reduce-scatter.2.cloned.1.call-update) | async-done | bytes 1048592 | tf_op jit(solution)/shard_map/reduce_scatter | solution.py:39
  310.7 1.5 all_to_all.18
  312.2 38.7 %all_to_all.25 = f32[64,4,1024]{2,1,0:T(4,128)S(1)} all-to-all(f32[64,4,1024]{2,1,0:T(4,128)S(1)} %all_to_all.18), channel_id=1, replica_groups=mesh['ab'=64,'cd'=4] {'ab'}, dimensions={0} | all-to-all | bytes 2097152 | tf_op jit(solution)/shard_map/all_to_all | solution.py:40
  350.9 1.0 copy.11
Async XLA Ops:
  6.5 304.1 %reduce-scatter.2.cloned.1.call-start = ((), (), s32[]{:S(2)}) async-start(), calls=%async_computation.3 | async-start | bytes 5242880 | tf_op jit(solution)/shard_map/reduce_scatter | solution.py:39
  206.1 4.9 %copy-start = (s32[2048]{0:T(1024)S(1)}, s32[2048]{0:T(1024)}, u32[]{:S(2)}) copy-start(s32[2048]{0:T(1024)} %param.9) | copy-start | bytes 24580
  206.1 4.9 %copy-start.1 = (s32[1024]{0:T(1024)S(1)}, s32[1024]{0:T(1024)}, u32[]{:S(2)}) copy-start(s32[1024]{0:T(1024)} %param.8) | copy-start | bytes 12292
Sparse Core Ops, SparseCore 0:
  263.7 46.9 reduce-scatter.1
